TPU v7x, 32 devices: a whole 2x2x4 slice. The times are simulated.
32 devices in a mesh: dp: 8 (over z, x), grp: 4 (over y, core).
Axes of the slice: x: 2, y: 2, z: 4, core: 2. Of those that a mesh axis runs over, the one named last changes fastest.
Arguments:
- down_in: bfloat16 [96, 32, 32, 160], P(('dp', 'grp')), may hold values from -6 to 6
- right_in: bfloat16 [96, 32, 32, 160], P(('dp', 'grp')), may hold values from -6 to 6
- pixel_mask: int32 [96, 32, 32], P(('dp', 'grp')), may hold values 0 or 1
- down_cot: bfloat16 [96, 32, 32, 160], P(('dp', 'grp')), may hold values from -6 to 6
- right_cot: bfloat16 [96, 32, 32, 160], P(('dp', 'grp')), may hold values from -6 to 6
- v_down1: bfloat16 [2, 1920, 160], P(None, 'dp'), may hold values from -0.125 to 0.125
- v_down2: bfloat16 [2, 1920, 320], P(None, 'dp'), may hold values from -0.125 to 0.125
- v_right1: bfloat16 [2, 1280, 160], P(None, 'dp'), may hold values from -0.15625 to 0.15625
- v_skip: bfloat16 [2, 320, 160], P(None, 'dp'), may hold values from -0.3125 to 0.3125
- v_right2: bfloat16 [2, 1280, 320], P(None, 'dp'), may hold values from -0.15625 to 0.15625
- gains: float32 [2, 1120], replicated, may hold values from 0.1 to 1.9
- biases: float32 [2, 1120], replicated, may hold values from -0.5 to 0.5
Outputs:
- down_out: bfloat16 [96, 32, 32, 160], P(('dp', 'grp'))
- right_out: bfloat16 [96, 32, 32, 160], P(('dp', 'grp'))
- down_grad: float32 [96, 32, 32, 160], P(('dp', 'grp'))
- right_grad: float32 [96, 32, 32, 160], P(('dp', 'grp'))
- grad_down1: float32 [2, 1920, 160], P(None, 'dp')
- grad_down2: float32 [2, 1920, 320], P(None, 'dp')
- grad_right1: float32 [2, 1280, 160], P(None, 'dp')
- grad_skip: float32 [2, 320, 160], P(None, 'dp')
- grad_right2: float32 [2, 1280, 320], P(None, 'dp')
- grad_gains: float32 [2, 1120], replicated
- grad_biases: float32 [2, 1120], replicated
Inputs may be any that keep to these rules, and one draw needn't show every extreme that they name: `pixel_mask`: 1 marks a counted pixel, 0 one that is not.
All inputs are finite; a program needn't handle non-finite values. No bound on the sum of `pixel_mask` on one device may be relied on, other than what follows from the above.
Results may differ from a plain program's by a relative error of at most 0.015.
Values may be sent and summed in bfloat16 or wider, within the bound.
A program may use at most 256 MiB of HBM per device.

v0:
```python
import jax
import jax.numpy as jnp
from jax import lax
from jax.sharding import PartitionSpec as P

LAYERS = 2


def span_list(filters):
    return [
        (0, filters),
        (filters, 3 * filters),
        (3 * filters, 4 * filters),
        (4 * filters, 5 * filters),
        (5 * filters, 7 * filters),
    ]


def tap_offsets(stencil):
    if stencil == "down":
        return [(row_off, col_off) for row_off in range(2) for col_off in range(3)]
    return [(row_off, col_off) for row_off in range(2) for col_off in range(2)]


def side_pad(stencil):
    return 2 if stencil == "down" else 1


def padded_cells(cells, stencil):
    return jnp.pad(cells, ((0, 0), (1, 0), (1, side_pad(stencil) - 1), (0, 0)))


def conv_apply(cells, weight, stencil):
    height, breadth, channels = (cells.shape[1], cells.shape[2], cells.shape[3])
    padded = padded_cells(cells, stencil)
    summed = None
    for tap_num, (row_off, col_off) in enumerate(tap_offsets(stencil)):
        window = padded[:, row_off : row_off + height, col_off : col_off + breadth, :]
        weight_tap = weight[tap_num * channels : (tap_num + 1) * channels]
        contrib = jnp.einsum(
            "bhwc,co->bhwo", window, weight_tap, preferred_element_type=jnp.float32
        )
        summed = contrib if summed is None else summed + contrib
    return summed


def conv_input_grad(grad_out, weight, stencil):
    breadth = grad_out.shape[2]
    offsets = tap_offsets(stencil)
    channels = weight.shape[0] // len(offsets)
    summed = None
    for tap_num, (row_off, col_off) in enumerate(offsets):
        weight_tap = weight[tap_num * channels : (tap_num + 1) * channels]
        contrib = jnp.einsum(
            "bhwo,co->bhwc", grad_out, weight_tap, preferred_element_type=jnp.float32
        )
        placed = jnp.pad(
            contrib,
            ((0, 0), (row_off, 1 - row_off), (col_off, side_pad(stencil) - col_off), (0, 0)),
        )
        summed = placed if summed is None else summed + placed
    return summed[:, 1:, 1 : 1 + breadth, :]


def conv_weight_grad(cells, grad_out, stencil):
    height, breadth = (cells.shape[1], cells.shape[2])
    padded = padded_cells(cells, stencil)
    pieces = []
    for row_off, col_off in tap_offsets(stencil):
        window = padded[:, row_off : row_off + height, col_off : col_off + breadth, :]
        pieces.append(
            jnp.einsum("bhwc,bhwo->co", window, grad_out, preferred_element_type=jnp.float32)
        )
    return jnp.concatenate(pieces, axis=0)


def pair_elu(values):
    return jax.nn.elu(jnp.concatenate([values, -values], axis=-1))


def elu_back(grad, source):
    channels = source.shape[-1]
    upper = jnp.where(source > 0, 1.0, jnp.exp(source))
    lower = jnp.where(source < 0, 1.0, jnp.exp(-source))
    return grad[..., :channels] * upper - grad[..., channels:] * lower


def gate_apply(flow, gate):
    channels = flow.shape[-1]
    return flow + gate[..., :channels] * jax.nn.sigmoid(gate[..., channels:])


def gate_back(grad, gate):
    channels = grad.shape[-1]
    top_half = gate[..., :channels]
    squash = jax.nn.sigmoid(gate[..., channels:])
    return jnp.concatenate(
        [grad * squash, grad * top_half * squash * (1.0 - squash)], axis=-1
    ).astype(jnp.bfloat16)


def prepare(whole, gains, spans):
    scaled = []
    inverse = []
    for full, (start_col, stop_col) in zip(whole, spans):
        values = full.astype(jnp.float32)
        recip = lax.rsqrt(jnp.sum(values * values, axis=1))
        scaled.append(
            (values * (gains[:, start_col:stop_col] * recip)[:, None, :]).astype(jnp.bfloat16)
        )
        inverse.append(recip)
    return (scaled, inverse)


def column_sum(grad):
    return jnp.sum(grad, axis=(0, 1, 2), dtype=jnp.float32)


def on_device(
    down_in,
    right_in,
    pixel_mask,
    down_cot,
    right_cot,
    v_down1,
    v_down2,
    v_right1,
    v_skip,
    v_right2,
    gains,
    biases,
):
    filters = down_in.shape[-1]
    spans = span_list(filters)
    shards = (v_down1, v_down2, v_right1, v_skip, v_right2)
    whole = (
        lax.all_gather(v_down1, "dp", axis=1, tiled=True),
        lax.all_gather(v_down2, "dp", axis=1, tiled=True),
        lax.all_gather(v_right1, "dp", axis=1, tiled=True),
        lax.all_gather(v_skip, "dp", axis=1, tiled=True),
        lax.all_gather(v_right2, "dp", axis=1, tiled=True),
    )
    scaled, inverse = prepare(whole, gains, spans)
    down_flow = down_in.astype(jnp.float32)
    right_flow = right_in.astype(jnp.float32)
    activated = pair_elu(down_flow).astype(jnp.bfloat16)
    kept = []
    for layer_num in range(LAYERS):
        weights = [scaled_now[layer_num] for scaled_now in scaled]
        bias_parts = [biases[layer_num, start_col:stop_col] for start_col, stop_col in spans]
        hidden_down = conv_apply(activated, weights[0], "down") + bias_parts[0]
        act_down = pair_elu(hidden_down).astype(jnp.bfloat16)
        gate_down = conv_apply(act_down, weights[1], "down") + bias_parts[1]
        new_down = gate_apply(down_flow, gate_down)
        new_act = pair_elu(new_down).astype(jnp.bfloat16)
        act_right = pair_elu(right_flow).astype(jnp.bfloat16)
        skip_term = jnp.einsum(
            "bhwk,ko->bhwo", new_act, weights[3], preferred_element_type=jnp.float32
        )
        hidden_right = (
            conv_apply(act_right, weights[2], "right") + skip_term + bias_parts[2] + bias_parts[3]
        )
        act_hidden = pair_elu(hidden_right).astype(jnp.bfloat16)
        gate_right = conv_apply(act_hidden, weights[4], "right") + bias_parts[4]
        new_right = gate_apply(right_flow, gate_right)
        kept.append(
            (
                down_flow,
                activated,
                hidden_down,
                act_down,
                gate_down,
                new_down,
                new_act,
                right_flow,
                act_right,
                hidden_right,
                act_hidden,
                gate_right,
            )
        )
        down_flow, right_flow, activated = (new_down, new_right, new_act)
    down_out = down_flow.astype(jnp.bfloat16)
    right_out = right_flow.astype(jnp.bfloat16)
    whole = (
        lax.all_gather(v_down1, "dp", axis=1, tiled=True),
        lax.all_gather(v_down2, "dp", axis=1, tiled=True),
        lax.all_gather(v_right1, "dp", axis=1, tiled=True),
        lax.all_gather(v_skip, "dp", axis=1, tiled=True),
        lax.all_gather(v_right2, "dp", axis=1, tiled=True),
    )
    scaled, inverse = prepare(whole, gains, spans)
    mask_float = pixel_mask.astype(jnp.float32)[..., None]
    grad_down = down_cot.astype(jnp.float32) * mask_float
    grad_right = right_cot.astype(jnp.float32) * mask_float
    grad_cells = jnp.zeros(grad_down.shape[:-1] + (2 * filters,), jnp.float32)
    layer_grads = [None] * LAYERS
    layer_bias = [None] * LAYERS
    for layer_num in reversed(range(LAYERS)):
        (
            down_flow,
            activated,
            hidden_down,
            act_down,
            gate_down,
            new_down,
            new_act,
            right_flow,
            act_right,
            hidden_right,
            act_hidden,
            gate_right,
        ) = kept[layer_num]
        weights = [scaled_now[layer_num] for scaled_now in scaled]
        grad_gate_right = gate_back(grad_right, gate_right)
        grad_w_right2 = conv_weight_grad(act_hidden, grad_gate_right, "right")
        grad_hid_right = elu_back(
            conv_input_grad(grad_gate_right, weights[4], "right"), hidden_right
        ).astype(jnp.bfloat16)
        grad_w_right1 = conv_weight_grad(act_right, grad_hid_right, "right")
        grad_w_skip = jnp.einsum(
            "bhwc,bhwo->co", new_act, grad_hid_right, preferred_element_type=jnp.float32
        )
        grad_cells = grad_cells + jnp.einsum(
            "bhwo,co->bhwc", grad_hid_right, weights[3], preferred_element_type=jnp.float32
        )
        grad_right = grad_right + elu_back(
            conv_input_grad(grad_hid_right, weights[2], "right"), right_flow
        )
        grad_down = grad_down + elu_back(grad_cells, new_down)
        grad_gate_down = gate_back(grad_down, gate_down)
        grad_w_down2 = conv_weight_grad(act_down, grad_gate_down, "down")
        grad_hid_down = elu_back(
            conv_input_grad(grad_gate_down, weights[1], "down"), hidden_down
        ).astype(jnp.bfloat16)
        grad_w_down1 = conv_weight_grad(activated, grad_hid_down, "down")
        grad_cells = conv_input_grad(grad_hid_down, weights[0], "down")
        layer_grads[layer_num] = (
            grad_w_down1,
            grad_w_down2,
            grad_w_right1,
            grad_w_skip,
            grad_w_right2,
        )
        right_bias = column_sum(grad_hid_right)
        layer_bias[layer_num] = jnp.concatenate(
            [
                column_sum(grad_hid_down),
                column_sum(grad_gate_down),
                right_bias,
                right_bias,
                column_sum(grad_gate_right),
            ]
        )
    down_grad = grad_down + elu_back(grad_cells, kept[0][0])
    local_grads = [
        jnp.stack([layer_grads[layer_num][map_num] for layer_num in range(LAYERS)])
        for map_num in range(5)
    ]
    bias_local = jnp.stack(layer_bias)
    row_sums = (
        lax.psum_scatter(local_grads[0], "dp", scatter_dimension=1, tiled=True),
        lax.psum_scatter(local_grads[1], "dp", scatter_dimension=1, tiled=True),
        lax.psum_scatter(local_grads[2], "dp", scatter_dimension=1, tiled=True),
        lax.psum_scatter(local_grads[3], "dp", scatter_dimension=1, tiled=True),
        lax.psum_scatter(local_grads[4], "dp", scatter_dimension=1, tiled=True),
    )
    group_sums = (
        lax.psum(row_sums[0].astype(jnp.bfloat16), "grp").astype(jnp.float32),
        lax.psum(row_sums[1].astype(jnp.bfloat16), "grp").astype(jnp.float32),
        lax.psum(row_sums[2].astype(jnp.bfloat16), "grp").astype(jnp.float32),
        lax.psum(row_sums[3].astype(jnp.bfloat16), "grp").astype(jnp.float32),
        lax.psum(row_sums[4].astype(jnp.bfloat16), "grp").astype(jnp.float32),
    )
    units = [
        shards[map_num].astype(jnp.float32) * inverse[map_num][:, None, :] for map_num in range(5)
    ]
    bias_sum = lax.psum(bias_local, ("dp", "grp"))
    dots_shard = jnp.concatenate(
        [jnp.sum(units[map_num] * group_sums[map_num], axis=1) for map_num in range(5)], axis=1
    )
    gain_sum = lax.psum(dots_shard, "dp")
    grad_dirs = []
    for map_num, (start_col, stop_col) in enumerate(spans):
        factor = (gains[:, start_col:stop_col] * inverse[map_num])[:, None, :]
        grad_dirs.append(
            factor * (group_sums[map_num] - units[map_num] * gain_sum[:, None, start_col:stop_col])
        )
    return (
        down_out,
        right_out,
        down_grad,
        grad_right,
        grad_dirs[0],
        grad_dirs[1],
        grad_dirs[2],
        grad_dirs[3],
        grad_dirs[4],
        gain_sum,
        bias_sum,
    )


def solution(mesh):
    placed = (
        P(("dp", "grp"), None, None, None),
        P(("dp", "grp"), None, None, None),
        P(("dp", "grp"), None, None),
        P(("dp", "grp"), None, None, None),
        P(("dp", "grp"), None, None, None),
        P(None, "dp", None),
        P(None, "dp", None),
        P(None, "dp", None),
        P(None, "dp", None),
        P(None, "dp", None),
        P(),
        P(),
    )
    return jax.shard_map(
        on_device,
        mesh=mesh,
        in_specs=placed,
        out_specs=(
            P(("dp", "grp"), None, None, None),
            P(("dp", "grp"), None, None, None),
            P(("dp", "grp"), None, None, None),
            P(("dp", "grp"), None, None, None),
            P(None, "dp", None),
            P(None, "dp", None),
            P(None, "dp", None),
            P(None, "dp", None),
            P(None, "dp", None),
            P(),
            P(),
        ),
        check_vma=False,
    )
```

profile of v0, /device:TPU:0, one launch (start us, length us, event | category | flops | bytes accessed | tf_op | source)
XLA Modules:
  0.0 1093.7 jit_solution(6300883025291663017)
XLA Ops:
  24.0 33.5 %all_gather.23 = bf16[2,320,160]{2,0,1:T(2,128)(2,1)S(1)} all-gather(bf16[2,40,160]{2,0,1:T(2,128)(2,1)S(1)} %copy.37), channel_id=1, replica_groups=mesh['dp'=8,'grp'=4] {'dp'}, dimensions={1}, use_global_device_ids=true | all-gather | bytes 230400 | tf_op jit(solution)/shard_map/all_gather | solution.py:140
  57.9 36.9 %all_gather.22 = bf16[2,1280,160]{2,0,1:T(2,128)(2,1)S(1)} all-gather(bf16[2,160,160]{2,0,1:T(2,128)(2,1)S(1)} %copy.35), channel_id=1, replica_groups=mesh['dp'=8,'grp'=4] {'dp'}, dimensions={1}, use_global_device_ids=true | all-gather | bytes 921600 | tf_op jit(solution)/shard_map/all_gather | solution.py:139
  97.0 5.3 fusion.3
  105.7 6.1 copy.33
  140.7 40.0 %all-gather.6.cloned.1.call-done = bf16[2,1920,320]{2,1,0:T(8,128)(2,1)} async-done(((bf16[2,240,320]{2,1,0:T(8,128)(2,1)}), bf16[2,1920,320]{2,1,0:T(8,128)(2,1)}) %all-gather.6.cloned.1.call-update) | async-done | bytes 2457616 | tf_op jit(solution)/shard_map/all_gather | solution.py:138
  197.4 3.9 fusion.69
  201.3 7.9 add_add_fusion.3
  223.7 5.4 fusion.292
  248.2 3.8 fusion.87
  252.0 4.3 fusion.293
  267.7 4.9 add_add_fusion.1
  288.1 9.1 add_add_fusion.2
  300.4 11.1 %convert_reduce_fusion.11 = (u32[3,32,160]{2,1,0:T(8,128)}, u32[3,32,160]{2,1,0:T(8,128)}, f32[3,32,32,160]{3,2,1,0:T(8,128)S(1)}) fusion(f32[160]{0:T(256)S(1)} %bitcast.665, f32[160]{0:T(256)S(1)} %bitcast.664, bf16[2,320,160]{1,2,0:T(8,128)(2,1)S(1)} %fusion.156, f32[3,32,32,160]{3,2,1,0:T(8,128)} %get-tuple-element.73, ...), kind=kOutput, calls=%fused_computation.101 | convolution fusion | flops 326338560 | bytes 15190016 | tf_op jit(solution)/shard_map/bhwk,ko->bhwo/dot_general | solution.py:157
  322.7 4.7 multiply_convert_fusion.7
  332.9 3.8 fusion.183
  344.2 11.0 %pad_add_fusion.6 = f32[3,33,33,320]{3,2,1,0:T(8,128)} fusion(f32[3,32,32,320]{3,2,1,0:T(8,128)} %fusion.184, f32[3,32,32,320]{3,2,1,0:T(8,128)} %fusion.183, f32[3,32,32,320]{3,2,1,0:T(8,128)} %fusion.182, f32[3,32,32,320]{3,2,1,0:T(8,128)} %fusion.181), kind=kLoop, calls=%fused_computation.26 | loop fusion | flops 3136320 | bytes 19910400 | tf_op jit(solution)/shard_map/add | solution.py:61
  355.2 6.4 convert_reduce_fusion.12
  383.7 11.1 %pad_add_fusion.4 = f32[3,33,33,320]{3,2,1,0:T(8,128)} fusion(f32[3,32,32,320]{3,2,1,0:T(8,128)} %fusion.207, f32[3,32,32,320]{3,2,1,0:T(8,128)} %fusion.206, f32[3,32,32,320]{3,2,1,0:T(8,128)} %fusion.205, f32[3,32,32,320]{3,2,1,0:T(8,128)} %fusion.204), kind=kLoop, calls=%fused_computation.24 | loop fusion | flops 3136320 | bytes 19910400 | tf_op jit(solution)/shard_map/add | solution.py:61
  394.8 14.6 %multiply_convert_fusion.3 = (bf16[3,32,32,160]{3,2,1,0:T(8,128)(2,1)S(1)}, f32[3,32,32,160]{3,2,1,0:T(8,128)S(1)}, bf16[3,32,32,160]{3,2,1,0:T(8,128)(2,1)}, bf...) fusion(f32[3,32,32,320]{3,2,1,0:T(8,128)} %copy-done.24, f32[3,32,32,160]{3,2,1,0:T(8,128)} %copy-done.39, ...), kind=kLoop, calls=%fused_computation.155 | loop fusion | flops 16220160 | bytes 24588288 | tf_op jit(solution)/shard_map/convert.2
  429.6 3.8 fusion.177
  433.4 11.0 %pad_add_fusion.3 = f32[3,33,33,320]{3,2,1,0:T(8,128)} fusion(f32[3,32,32,320]{3,2,1,0:T(8,128)} %fusion.180, f32[3,32,32,320]{3,2,1,0:T(8,128)} %fusion.179, f32[3,32,32,320]{3,2,1,0:T(8,128)} %fusion.178, f32[3,32,32,320]{3,2,1,0:T(8,128)} %fusion.177), kind=kLoop, calls=%fused_computation.23 | loop fusion | flops 3136320 | bytes 19910400 | tf_op jit(solution)/shard_map/add | solution.py:61
  444.5 6.5 convert_reduce_fusion.14
  471.7 4.0 fusion.170
  475.7 8.8 pad_add_fusion.5
  514.3 12.8 %fusion.20 = f32[3,32,32,320]{3,2,1,0:T(8,128)} fusion(f32[3,32,32,320]{3,2,1,0:T(8,128)} %fusion.198, f32[3,32,32,320]{3,2,1,0:T(8,128)} %fusion.196, f32[3,32,32,320]{3,2,1,0:T(8,128)} %fusion.195, f32[3,32,32,320]{3,2,1,0:T(8,128)} %fusion.194, f32[3,32,32,320]{3,2,1,0:T(8,128)} %fusion.193, f32[3,32,32,320]{3,2,1,0:T(8,128)} %fusion.192, ...), kind=kOutput, calls=%fused_computation.51 | convolution fusion | flops 320471040 | bytes 29220864 | tf_op jit(solution)/shard_map/bhwo,co->bhwc/dot_general | solution.py:224
  528.1 4.7 multiply_convert_fusion.1
  543.9 3.8 fusion.166
  565.2 4.7 copy.135
  570.0 4.4 reshape.186
  574.5 3.9 fusion.147
  580.6 10.7 pad_add_fusion.2
  606.4 6.7 copy.131
  613.0 6.0 reshape.182
  635.2 4.8 concatenate.92
  652.7 4.4 concatenate.91
  657.1 4.3 pad_maximum_fusion
  661.4 9.8 copy.133
  671.2 8.1 reshape.184
  692.3 3.9 fusion.124
  706.4 7.6 copy.43
  716.4 5.7 convolution_bitcast_fusion.4
  724.2 212.3 %all-reduce.56 = (bf16[2,320,160]{2,0,1:T(2,128)(2,1)S(1)}, bf16[2,1280,320]{2,0,1:T(2,128)(2,1)}) all-reduce(f32[2,320,160]{2,0,1:T(2,128)S(1)} %copy.41, f32[2,1280,320]{2,0,1:T(2,128)} %copy.43), channel_id=5, replica_groups=mesh['dp'=8,'grp'=4] {'dp'}, use_global_device_ids=true, to_apply=%region_14.15.clone | all-reduce | flops 921600 | bytes 5529600
  951.0 11.1 %pad_add_fusion = f32[3,33,33,320]{3,2,1,0:T(8,128)} fusion(f32[3,32,32,320]{3,2,1,0:T(8,128)} %fusion.202, f32[3,32,32,320]{3,2,1,0:T(8,128)} %fusion.201, f32[3,32,32,320]{3,2,1,0:T(8,128)} %fusion.200, f32[3,32,32,320]{3,2,1,0:T(8,128)} %fusion.199), kind=kLoop, calls=%fused_computation.20 | loop fusion | flops 3136320 | bytes 19910400 | tf_op jit(solution)/shard_map/add | solution.py:61
  978.9 10.2 pad_add_fusion.1
  992.9 3.8 fusion.26
  1003.6 39.0 %psum.55 = f32[2,1120]{1,0:T(2,128)} all-reduce(f32[2,1120]{1,0:T(2,128)S(1)} %pad_maximum_fusion.9), channel_id=1, replica_groups=mesh['dp'=8,'grp'=4] {'dp','grp'}, use_global_device_ids=true, to_apply=%region_29.30 | all-reduce | flops 2240 | bytes 17920 | tf_op jit(solution)/shard_map/psum | solution.py:278
  1042.7 11.6 %psum.52 = bf16[2,40,160]{2,0,1:T(2,128)(2,1)S(1)} all-reduce(bf16[2,40,160]{2,0,1:T(2,128)(2,1)S(1)} %dynamic-slice_convert_fusion.1), channel_id=1, replica_groups=mesh['dp'=8,'grp'=4] {'grp'}, use_global_device_ids=true, to_apply=%region_15.16 | all-reduce | flops 12800 | bytes 51200 | tf_op jit(solution)/shard_map/psum | solution.py:272
  1059.7 20.5 %psum.54 = f32[2,1120]{1,0:T(2,128)S(1)} all-reduce(f32[2,1120]{1,0:T(2,128)S(1)} %concatenate.97), channel_id=1, replica_groups=mesh['dp'=8,'grp'=4] {'dp'}, use_global_device_ids=true, to_apply=%region_20.21 | all-reduce | flops 2240 | bytes 17920 | tf_op jit(solution)/shard_map/psum | solution.py:282
  (488 shorter events, 403.5 us)
Async XLA Ops:
  7.2 98.6 %all-gather.4.cloned.1.call-start = ((), (), s32[]{:S(2)}) async-start(), calls=%async_computation.3 | async-start | bytes 2211840 | tf_op jit(solution)/shard_map/all_gather | solution.py:137
  9.1 129.5 %all-gather.8.cloned.1.call-start = ((), (), s32[]{:S(2)}) async-start(), calls=%async_computation.5 | async-start | bytes 2211840 | tf_op jit(solution)/shard_map/all_gather | solution.py:141
  9.9 170.8 %all-gather.6.cloned.1.call-start = ((), (), s32[]{:S(2)}) async-start(), calls=%async_computation.4 | async-start | bytes 3317760 | tf_op jit(solution)/shard_map/all_gather | solution.py:138
  11.8 985.0 %reduce-scatter.14.cloned.1.call-start = ((), (), s32[]{:S(2)}) async-start(), calls=%async_computation.8 | async-start | bytes 2211840
  102.3 18.7 %copy-start.16 = (bf16[3,32,32,320]{3,2,1,0:T(8,128)(2,1)}, bf16[3,32,32,320]{3,2,1,0:T(8,128)(2,1)S(1)}, u32[]{:S(2)}) copy-start(bf16[3,32,32,320]{3,2,1,0:T(8,128)(2,1)S(1)} %fusion.3) | copy-start | bytes 5898244
  114.1 12.1 %copy-start.110 = (f32[2,160]{1,0:T(2,128)}, f32[2,160]{1,0:T(2,128)S(1)}, u32[]{:S(2)}) copy-start(f32[2,160]{1,0:T(2,128)S(1)} %get-tuple-element.100) | copy-start | bytes 3844
  124.6 76.7 %copy-start.18 = (bf16[3,32,32,320]{3,2,1,0:T(8,128)(2,1)}, bf16[3,32,32,320]{3,2,1,0:T(8,128)(2,1)S(1)}, u32[]{:S(2)}) copy-start(bf16[3,32,32,320]{3,2,1,0:T(8,128)(2,1)S(1)} %fusion.5) | copy-start | bytes 5898244
  127.4 250.1 %copy-start.69 = (bf16[2,1280,160]{1,2,0:T(8,128)(2,1)}, bf16[2,1280,160]{1,2,0:T(8,128)(2,1)S(1)}, u32[]{:S(2)}) copy-start(bf16[2,1280,160]{1,2,0:T(8,128)(2,1)S(1)} %fusion.120) | copy-start | bytes 2457604
  183.9 76.4 %copy-start.102 = (f32[2,320]{1,0:T(2,128)}, f32[2,320]{1,0:T(2,128)S(1)}, u32[]{:S(2)}) copy-start(f32[2,320]{1,0:T(2,128)S(1)} %get-tuple-element.97) | copy-start | bytes 7684
  184.5 103.5 %copy-start.47 = (bf16[2,1920,320]{2,1,0:T(8,128)(2,1)}, bf16[2,1920,320]{2,1,0:T(8,128)(2,1)S(1)}, u32[]{:S(2)}) copy-start(bf16[2,1920,320]{2,1,0:T(8,128)(2,1)S(1)} %fusion.1) | copy-start | bytes 7372804
  211.4 85.7 %copy-start.33 = (f32[3,32,32,160]{3,2,1,0:T(8,128)}, f32[3,32,32,160]{3,2,1,0:T(8,128)S(1)}, u32[]{:S(2)}) copy-start(f32[3,32,32,160]{3,2,1,0:T(8,128)S(1)} %get-tuple-element.78) | copy-start | bytes 5898244
  213.6 38.4 %copy-start.5 = (bf16[3,32,32,320]{3,2,1,0:T(8,128)(2,1)}, bf16[3,32,32,320]{3,2,1,0:T(8,128)(2,1)S(1)}, u32[]{:S(2)}) copy-start(bf16[3,32,32,320]{3,2,1,0:T(8,128)(2,1)S(1)} %fusion.7) | copy-start | bytes 5898244
  233.2 54.8 %copy-start.20 = (bf16[3,32,32,320]{3,2,1,0:T(8,128)(2,1)}, bf16[3,32,32,320]{3,2,1,0:T(8,128)(2,1)S(1)}, u32[]{:S(2)}) copy-start(bf16[3,32,32,320]{3,2,1,0:T(8,128)(2,1)S(1)} %fusion.9) | copy-start | bytes 5898244
  274.7 48.0 %copy-start.39 = (f32[3,32,32,160]{3,2,1,0:T(8,128)}, f32[3,32,32,160]{3,2,1,0:T(8,128)S(1)}, u32[]{:S(2)}) copy-start(f32[3,32,32,160]{3,2,1,0:T(8,128)S(1)} %get-tuple-element.76) | copy-start | bytes 5898244
  361.6 19.0 %copy-start.12 = (bf16[3,32,32,160]{3,2,1,0:T(8,128)(2,1)}, bf16[3,32,32,160]{3,2,1,0:T(8,128)(2,1)S(1)}, u32[]{:S(2)}) copy-start(bf16[3,32,32,160]{3,2,1,0:T(8,128)(2,1)S(1)} %get-tuple-element.62) | copy-start | bytes 2949124
  383.7 25.7 %slice-start.2 = ((s8[4718592]{0:T(1024)(128)(4,1)}), s8[524288]{0:T(1024)(128)(4,1)S(1)}, s32[]{:S(2)}) async-start(s8[4718592]{0:T(1024)(128)(4,1)} %bitcast.644), calls=%async_computation.12 | async-start | bytes 1048576
  394.8 14.6 %slice-start.3 = ((s8[4718592]{0:T(1024)(128)(4,1)}), s8[4194304]{0:T(1024)(128)(4,1)S(1)}, s32[]{:S(2)}) async-start(s8[4718592]{0:T(1024)(128)(4,1)} %bitcast.644), calls=%async_computation.13 | async-start | bytes 8388608
  451.0 63.3 %copy-start.14 = (bf16[3,32,32,160]{3,2,1,0:T(8,128)(2,1)}, bf16[3,32,32,160]{3,2,1,0:T(8,128)(2,1)S(1)}, u32[]{:S(2)}) copy-start(bf16[3,32,32,160]{3,2,1,0:T(8,128)(2,1)S(1)} %get-tuple-element.54) | copy-start | bytes 2949124
  487.5 23.7 %copy-start.4 = (bf16[3,32,32,160]{3,2,1,0:T(8,128)(2,1)}, bf16[3,32,32,160]{3,2,1,0:T(8,128)(2,1)S(1)}, u32[]{:S(2)}) copy-start(bf16[3,32,32,160]{3,2,1,0:T(8,128)(2,1)S(1)} %get-tuple-element.66) | copy-start | bytes 2949124
  511.2 15.9 %slice-start = ((s8[4718592]{0:T(1024)(128)(4,1)}), s8[524288]{0:T(1024)(128)(4,1)S(1)}, s32[]{:S(2)}) async-start(s8[4718592]{0:T(1024)(128)(4,1)} %bitcast.642), calls=%async_computation.10 | async-start | bytes 1048576
  514.3 12.8 %slice-start.1 = ((s8[4718592]{0:T(1024)(128)(4,1)}), s8[4194304]{0:T(1024)(128)(4,1)S(1)}, s32[]{:S(2)}) async-start(s8[4718592]{0:T(1024)(128)(4,1)} %bitcast.642), calls=%async_computation.11 | async-start | bytes 8388608
  514.3 12.8 %copy-start.34 = (f32[3,32,32,160]{3,2,1,0:T(8,128)S(1)}, f32[3,32,32,160]{3,2,1,0:T(8,128)}, u32[]{:S(2)}) copy-start(f32[3,32,32,160]{3,2,1,0:T(8,128)} %copy-done.33) | copy-start | bytes 5898244
  514.3 13.8 %copy-start.45 = (f32[3,32,32,160]{3,2,1,0:T(8,128)S(1)}, f32[3,32,32,160]{3,2,1,0:T(8,128)}, u32[]{:S(2)}) copy-start(f32[3,32,32,160]{3,2,1,0:T(8,128)} %copy-done.44) | copy-start | bytes 5898244
  535.7 19.4 %copy-start = (bf16[3,32,32,320]{3,2,1,0:T(8,128)(2,1)}, bf16[3,32,32,320]{3,2,1,0:T(8,128)(2,1)S(1)}, u32[]{:S(2)}) copy-start(bf16[3,32,32,320]{3,2,1,0:T(8,128)(2,1)S(1)} %get-tuple-element.56) | copy-start | bytes 5898244
  574.4 424.4 %reduce-scatter.10.cloned.1.call-start = ((), (), s32[]{:S(2)}) async-start(), calls=%async_computation.6 | async-start | bytes 3317760
  619.0 381.8 %reduce-scatter.12.cloned.1.call-start = ((), (), s32[]{:S(2)}) async-start(), calls=%async_computation.7 | async-start | bytes 5529600
  682.3 372.2 %all-reduce.55.cloned.1.call-start = ((), (), s32[]{:S(2)}) async-start(), calls=%async_computation.9 | async-start | bytes 1802240 | tf_op jit(solution)/shard_map/psum | solution.py:269
  722.1 216.2 %copy-start.15 = (bf16[3,32,32,160]{3,2,1,0:T(8,128)(2,1)S(1)}, bf16[3,32,32,160]{3,2,1,0:T(8,128)(2,1)}, u32[]{:S(2)}) copy-start(bf16[3,32,32,160]{3,2,1,0:T(8,128)(2,1)} %copy-done.14) | copy-start | bytes 2949124
  722.1 216.2 %copy-start.70 = (bf16[2,1280,160]{1,2,0:T(8,128)(2,1)S(1)}, bf16[2,1280,160]{1,2,0:T(8,128)(2,1)}, u32[]{:S(2)}) copy-start(bf16[2,1280,160]{1,2,0:T(8,128)(2,1)} %copy-done.69) | copy-start | bytes 2457604
  975.8 13.3 %slice-start.6 = ((s8[6082560]{0:T(1024)(128)(4,1)}), s8[4194304]{0:T(1024)(128)(4,1)S(1)}, s32[]{:S(2)}) async-start(s8[6082560]{0:T(1024)(128)(4,1)} %bitcast.648), calls=%async_computation.16 | async-start | bytes 8388608
  996.7 57.6 %copy-start.93 = (bf16[2,40,160]{2,1,0:T(8,128)(2,1)S(1)}, bf16[2,40,160]{2,1,0:T(8,128)(2,1)}, u32[]{:S(2)}) copy-start(bf16[2,40,160]{2,1,0:T(8,128)(2,1)} %param.20) | copy-start | bytes 76804
  996.7 57.6 %copy-start.112 = (f32[2,160]{1,0:T(2,128)S(1)}, f32[2,160]{1,0:T(2,128)}, u32[]{:S(2)}) copy-start(f32[2,160]{1,0:T(2,128)} %get-tuple-element.106) | copy-start | bytes 3844
  996.7 57.7 %copy-start.78 = (bf16[2,240,160]{1,2,0:T(8,128)(2,1)S(1)}, bf16[2,240,160]{1,2,0:T(8,128)(2,1)}, u32[]{:S(2)}) copy-start(bf16[2,240,160]{1,2,0:T(8,128)(2,1)} %param.17) | copy-start | bytes 460804
  996.7 57.7 %copy-start.113 = (f32[2,160]{1,0:T(2,128)S(1)}, f32[2,160]{1,0:T(2,128)}, u32[]{:S(2)}) copy-start(f32[2,160]{1,0:T(2,128)} %get-tuple-element.104) | copy-start | bytes 3844
  996.7 59.0 %copy-start.76 = (bf16[2,240,320]{1,2,0:T(8,128)(2,1)S(1)}, bf16[2,240,320]{1,2,0:T(8,128)(2,1)}, u32[]{:S(2)}) copy-start(bf16[2,240,320]{1,2,0:T(8,128)(2,1)} %param.18) | copy-start | bytes 921604
  996.7 59.0 %copy-start.107 = (f32[2,320]{1,0:T(2,128)S(1)}, f32[2,320]{1,0:T(2,128)}, u32[]{:S(2)}) copy-start(f32[2,320]{1,0:T(2,128)} %get-tuple-element.102) | copy-start | bytes 7684
  996.7 60.3 %copy-start.77 = (bf16[2,160,320]{2,1,0:T(8,128)(2,1)S(1)}, bf16[2,160,320]{2,1,0:T(8,128)(2,1)}, u32[]{:S(2)}) copy-start(bf16[2,160,320]{2,1,0:T(8,128)(2,1)} %param.21) | copy-start | bytes 614404
  996.8 60.3 %copy-start.104 = (f32[2,320]{1,0:T(2,128)S(1)}, f32[2,320]{1,0:T(2,128)}, u32[]{:S(2)}) copy-start(f32[2,320]{1,0:T(2,128)} %get-tuple-element.103) | copy-start | bytes 7684
  996.8 61.7 %copy-start.79 = (bf16[2,160,160]{1,2,0:T(8,128)(2,1)S(1)}, bf16[2,160,160]{1,2,0:T(8,128)(2,1)}, u32[]{:S(2)}) copy-start(bf16[2,160,160]{1,2,0:T(8,128)(2,1)} %copy.39) | copy-start | bytes 307204
  996.8 61.6 %copy-start.114 = (f32[2,160]{1,0:T(2,128)S(1)}, f32[2,160]{1,0:T(2,128)}, u32[]{:S(2)}) copy-start(f32[2,160]{1,0:T(2,128)} %get-tuple-element.105) | copy-start | bytes 3844
  998.0 82.4 %copy-start.111 = (f32[2,160]{1,0:T(2,128)S(1)}, f32[2,160]{1,0:T(2,128)}, u32[]{:S(2)}) copy-start(f32[2,160]{1,0:T(2,128)} %copy-done.110) | copy-start | bytes 3844
  1000.8 81.6 %copy-start.109 = (f32[2,160]{1,0:T(2,128)S(1)}, f32[2,160]{1,0:T(2,128)}, u32[]{:S(2)}) copy-start(f32[2,160]{1,0:T(2,128)} %copy-done.108) | copy-start | bytes 3844
  1000.8 82.3 %copy-start.116 = (f32[2,160]{1,0:T(2,128)S(1)}, f32[2,160]{1,0:T(2,128)}, u32[]{:S(2)}) copy-start(f32[2,160]{1,0:T(2,128)} %copy-done.115) | copy-start | bytes 3844
  1002.2 81.8 %copy-start.103 = (f32[2,320]{1,0:T(2,128)S(1)}, f32[2,320]{1,0:T(2,128)}, u32[]{:S(2)}) copy-start(f32[2,320]{1,0:T(2,128)} %copy-done.102) | copy-start | bytes 7684
  1054.4 28.7 %copy-start.84 = (bf16[2,240,160]{1,2,0:T(8,128)(2,1)S(1)}, bf16[2,240,160]{1,2,0:T(8,128)(2,1)}, u32[]{:S(2)}) copy-start(bf16[2,240,160]{1,2,0:T(8,128)(2,1)} %get-tuple-element.47) | copy-start | bytes 460804
  1054.4 29.6 %copy-start.81 = (bf16[2,160,320]{2,0,1:T(2,128)(2,1)S(1)}, bf16[2,160,320]{2,0,1:T(2,128)(2,1)}, u32[]{:S(2)}) copy-start(bf16[2,160,320]{2,0,1:T(2,128)(2,1)} %get-tuple-element.50) | copy-start | bytes 614404
  1054.5 30.8 %copy-start.80 = (bf16[2,240,320]{1,2,0:T(8,128)(2,1)S(1)}, bf16[2,240,320]{1,2,0:T(8,128)(2,1)}, u32[]{:S(2)}) copy-start(bf16[2,240,320]{1,2,0:T(8,128)(2,1)} %get-tuple-element.48) | copy-start | bytes 921604
  1054.5 30.8 %copy-start.106 = (f32[2,320]{1,0:T(2,128)S(1)}, f32[2,320]{1,0:T(2,128)}, u32[]{:S(2)}) copy-start(f32[2,320]{1,0:T(2,128)} %copy-done.105) | copy-start | bytes 7684
  (91 other events, 455.1 us)
Sparse Core Ops, SparseCore 0:
  10.8 57.5 all-gather.3
  70.6 49.5 all-gather.7
  123.0 57.5 all-gather.5
  574.5 65.3 reduce-scatter.13
  643.7 71.8 reduce-scatter.9
  719.1 166.6 reduce-scatter.11
  1003.7 34.4 all-reduce.54
where the time goes:
time: 1100 us; the launch traced here: 1090 us
  matrix products  364 us (33%)
  blocking collectives  354 us (32%)
  other arithmetic  207 us (19%)
  local copies, waits for them, and re-layouts  110 us (10%)
  waiting for transfers between devices  40.8 us (4%)
  between operations  17.5 us (2%)
    unnamed x1, blocking collectives  212 us
    dot_general x40, matrix products, conv_input_grad(): jnp.einsum('bhwo,co->bhwc', grad_out, weight_tap, preferred_element_type=...  132 us
    dot_general x40, matrix products, conv_apply(): jnp.einsum('bhwc,co->bhwo', window, weight_tap, preferred_element_type=jn...  116 us
    dot_general x40, matrix products, conv_weight_grad(): jnp.einsum('bhwc,bhwo->co', window, grad_out, preferred_element_type=jnp....  76.2 us
    add x7, other arithmetic, conv_input_grad(): summed = placed if summed is None else summed + placed  73.9 us
    unnamed x285, local copies, waits for them, and re-layouts  65.9 us
    all_gather x1, waiting for transfers between devices, on_device(): lax.all_gather(v_down2, 'dp', axis=1, tiled=True)  40 us
    psum x1, blocking collectives, on_device(): bias_sum = lax.psum(bias_local, ('dp', 'grp'))  39 us
  transfers between devices with their start and end apart: 7, of which 1 were waited for; matrix products, arithmetic and copies ran while one was open for 25% of the time, Pallas kernels for 0%

commit v1 on v0

--- a/solution.py
+++ b/solution.py
@@ -275,7 +275,7 @@
     units = [
         shards[map_num].astype(jnp.float32) * inverse[map_num][:, None, :] for map_num in range(5)
     ]
-    bias_sum = lax.psum(bias_local, ("dp", "grp"))
+    bias_sum = lax.psum(lax.psum(bias_local, "grp"), "dp")
     dots_shard = jnp.concatenate(
         [jnp.sum(units[map_num] * group_sums[map_num], axis=1) for map_num in range(5)], axis=1
     )

time: 1100 us -> 1100 us (level)
  waiting for transfers between devices: 40.8 us -> 57 us
  blocking collectives: 354 us -> 338 us
    psum x1, blocking collectives: 39 us -> 7.7 us  [on_device(): bias_sum = lax.psum(lax.psum(bias_local, 'grp'), 'dp')]
    psum x1, blocking collectives: 20.5 us -> 37.7 us  [on_device(): gain_sum = lax.psum(dots_shard, 'dp')]
    psum x1, waiting for transfers between devices: 0.02 us -> 16.9 us  [on_device(): lax.psum(row_sums[0].astype(jnp.bfloat16), 'grp').astype(jnp.float32)]
  transfers between devices with their start and end apart: 7 -> 7, of which waited for: 1 -> 2; matrix products, arithmetic and copies ran while one was open for 25% -> 25% of each run, Pallas kernels for 0% -> 0%
where the time goes in v1:
time: 1100 us; the launch traced here: 1090 us
  matrix products  363 us (33%)
  blocking collectives  338 us (31%)
  other arithmetic  208 us (19%)
  local copies, waits for them, and re-layouts  110 us (10%)
  waiting for transfers between devices  57 us (5%)
  between operations  17.4 us (2%)
    unnamed x1, blocking collectives  210 us
    dot_general x40, matrix products, conv_input_grad(): jnp.einsum('bhwo,co->bhwc', grad_out, weight_tap, preferred_element_type=...  132 us
    dot_general x40, matrix products, conv_apply(): jnp.einsum('bhwc,co->bhwo', window, weight_tap, preferred_element_type=jn...  116 us
    dot_general x40, matrix products, conv_weight_grad(): jnp.einsum('bhwc,bhwo->co', window, grad_out, preferred_element_type=jnp....  76.2 us
    add x7, other arithmetic, conv_input_grad(): summed = placed if summed is None else summed + placed  73.9 us
    unnamed x285, local copies, waits for them, and re-layouts  65.9 us
    all_gather x1, waiting for transfers between devices, on_device(): lax.all_gather(v_down2, 'dp', axis=1, tiled=True)  39.2 us
    psum x1, blocking collectives, on_device(): gain_sum = lax.psum(dots_shard, 'dp')  37.7 us
  transfers between devices with their start and end apart: 7, of which 2 were waited for; matrix products, arithmetic and copies ran while one was open for 25% of the time, Pallas kernels for 0%

profile of v1, /device:TPU:0, one launch (start us, length us, event | category | flops | bytes accessed | tf_op | source)
XLA Modules:
  0.0 1094.3 jit_solution(13506643902203507373)
XLA Ops:
  24.0 33.5 %all_gather.23 = bf16[2,320,160]{2,0,1:T(2,128)(2,1)S(1)} all-gather(bf16[2,40,160]{2,0,1:T(2,128)(2,1)S(1)} %copy.37), channel_id=1, replica_groups=mesh['dp'=8,'grp'=4] {'dp'}, dimensions={1}, use_global_device_ids=true | all-gather | bytes 230400 | tf_op jit(solution)/shard_map/all_gather | solution.py:140
  57.9 37.5 %all_gather.22 = bf16[2,1280,160]{2,0,1:T(2,128)(2,1)S(1)} all-gather(bf16[2,160,160]{2,0,1:T(2,128)(2,1)S(1)} %copy.35), channel_id=1, replica_groups=mesh['dp'=8,'grp'=4] {'dp'}, dimensions={1}, use_global_device_ids=true | all-gather | bytes 921600 | tf_op jit(solution)/shard_map/all_gather | solution.py:139
  97.4 5.3 fusion.3
  106.2 6.1 copy.33
  141.2 39.2 %all-gather.6.cloned.1.call-done = bf16[2,1920,320]{2,1,0:T(8,128)(2,1)} async-done(((bf16[2,240,320]{2,1,0:T(8,128)(2,1)}), bf16[2,1920,320]{2,1,0:T(8,128)(2,1)}) %all-gather.6.cloned.1.call-update) | async-done | bytes 2457616 | tf_op jit(solution)/shard_map/all_gather | solution.py:138
  197.2 3.9 fusion.69
  201.1 7.9 add_add_fusion.3
  223.4 5.4 fusion.292
  247.9 3.8 fusion.87
  251.8 4.3 fusion.293
  267.4 4.9 add_add_fusion.1
  287.8 9.1 add_add_fusion.2
  300.1 11.1 %convert_reduce_fusion.11 = (u32[3,32,160]{2,1,0:T(8,128)}, u32[3,32,160]{2,1,0:T(8,128)}, f32[3,32,32,160]{3,2,1,0:T(8,128)S(1)}) fusion(f32[160]{0:T(256)S(1)} %bitcast.665, f32[160]{0:T(256)S(1)} %bitcast.664, bf16[2,320,160]{1,2,0:T(8,128)(2,1)S(1)} %fusion.156, f32[3,32,32,160]{3,2,1,0:T(8,128)} %get-tuple-element.75, ...), kind=kOutput, calls=%fused_computation.101 | convolution fusion | flops 326338560 | bytes 15190016 | tf_op jit(solution)/shard_map/bhwk,ko->bhwo/dot_general | solution.py:157
  322.4 4.7 multiply_convert_fusion.7
  332.6 3.8 fusion.183
  343.9 11.0 %pad_add_fusion.6 = f32[3,33,33,320]{3,2,1,0:T(8,128)} fusion(f32[3,32,32,320]{3,2,1,0:T(8,128)} %fusion.184, f32[3,32,32,320]{3,2,1,0:T(8,128)} %fusion.183, f32[3,32,32,320]{3,2,1,0:T(8,128)} %fusion.182, f32[3,32,32,320]{3,2,1,0:T(8,128)} %fusion.181), kind=kLoop, calls=%fused_computation.26 | loop fusion | flops 3136320 | bytes 19910400 | tf_op jit(solution)/shard_map/add | solution.py:61
  354.9 6.4 convert_reduce_fusion.12
  383.4 11.1 %pad_add_fusion.4 = f32[3,33,33,320]{3,2,1,0:T(8,128)} fusion(f32[3,32,32,320]{3,2,1,0:T(8,128)} %fusion.207, f32[3,32,32,320]{3,2,1,0:T(8,128)} %fusion.206, f32[3,32,32,320]{3,2,1,0:T(8,128)} %fusion.205, f32[3,32,32,320]{3,2,1,0:T(8,128)} %fusion.204), kind=kLoop, calls=%fused_computation.24 | loop fusion | flops 3136320 | bytes 19910400 | tf_op jit(solution)/shard_map/add | solution.py:61
  394.5 15.0 %multiply_convert_fusion.3 = (bf16[3,32,32,160]{3,2,1,0:T(8,128)(2,1)S(1)}, f32[3,32,32,160]{3,2,1,0:T(8,128)S(1)}, bf16[3,32,32,160]{3,2,1,0:T(8,128)(2,1)}, bf...) fusion(f32[3,32,32,320]{3,2,1,0:T(8,128)} %copy-done.24, f32[3,32,32,160]{3,2,1,0:T(8,128)} %copy-done.39, ...), kind=kLoop, calls=%fused_computation.155 | loop fusion | flops 16220160 | bytes 24588288 | tf_op jit(solution)/shard_map/convert.2
  429.7 3.8 fusion.177
  433.6 11.0 %pad_add_fusion.3 = f32[3,33,33,320]{3,2,1,0:T(8,128)} fusion(f32[3,32,32,320]{3,2,1,0:T(8,128)} %fusion.180, f32[3,32,32,320]{3,2,1,0:T(8,128)} %fusion.179, f32[3,32,32,320]{3,2,1,0:T(8,128)} %fusion.178, f32[3,32,32,320]{3,2,1,0:T(8,128)} %fusion.177), kind=kLoop, calls=%fused_computation.23 | loop fusion | flops 3136320 | bytes 19910400 | tf_op jit(solution)/shard_map/add | solution.py:61
  444.6 6.5 convert_reduce_fusion.14
  471.9 4.0 fusion.170
  475.8 8.8 pad_add_fusion.5
  514.3 12.8 %fusion.20 = f32[3,32,32,320]{3,2,1,0:T(8,128)} fusion(f32[3,32,32,320]{3,2,1,0:T(8,128)} %fusion.198, f32[3,32,32,320]{3,2,1,0:T(8,128)} %fusion.196, f32[3,32,32,320]{3,2,1,0:T(8,128)} %fusion.195, f32[3,32,32,320]{3,2,1,0:T(8,128)} %fusion.194, f32[3,32,32,320]{3,2,1,0:T(8,128)} %fusion.193, f32[3,32,32,320]{3,2,1,0:T(8,128)} %fusion.192, ...), kind=kOutput, calls=%fused_computation.51 | convolution fusion | flops 320471040 | bytes 29220864 | tf_op jit(solution)/shard_map/bhwo,co->bhwc/dot_general | solution.py:224
  528.1 4.7 multiply_convert_fusion.1
  565.3 4.7 copy.135
  570.1 4.4 reshape.186
  574.5 3.9 fusion.147
  580.6 10.7 pad_add_fusion.2
  606.4 6.7 copy.131
  613.1 6.0 reshape.182
  635.3 4.8 concatenate.92
  652.7 4.4 concatenate.91
  657.1 4.3 pad_maximum_fusion
  661.3 9.8 copy.133
  671.2 8.1 reshape.184
  692.3 3.9 fusion.124
  706.5 7.6 copy.43
  716.4 5.7 convolution_bitcast_fusion.4
  724.2 210.3 %all-reduce.57 = (bf16[2,320,160]{2,0,1:T(2,128)(2,1)S(1)}, bf16[2,1280,320]{2,0,1:T(2,128)(2,1)}) all-reduce(f32[2,320,160]{2,0,1:T(2,128)S(1)} %copy.41, f32[2,1280,320]{2,0,1:T(2,128)} %copy.43), channel_id=5, replica_groups=mesh['dp'=8,'grp'=4] {'dp'}, use_global_device_ids=true, to_apply=%region_14.15.clone | all-reduce | flops 921600 | bytes 5529600
  949.0 11.1 %pad_add_fusion = f32[3,33,33,320]{3,2,1,0:T(8,128)} fusion(f32[3,32,32,320]{3,2,1,0:T(8,128)} %fusion.202, f32[3,32,32,320]{3,2,1,0:T(8,128)} %fusion.201, f32[3,32,32,320]{3,2,1,0:T(8,128)} %fusion.200, f32[3,32,32,320]{3,2,1,0:T(8,128)} %fusion.199), kind=kLoop, calls=%fused_computation.20 | loop fusion | flops 3136320 | bytes 19910400 | tf_op jit(solution)/shard_map/add | solution.py:61
  976.9 10.2 pad_add_fusion.1
  990.8 3.8 fusion.26
  1001.6 7.7 psum.62
  1009.3 11.5 %psum.59 = bf16[2,40,160]{2,0,1:T(2,128)(2,1)S(1)} all-reduce(bf16[2,40,160]{2,0,1:T(2,128)(2,1)S(1)} %dynamic-slice_convert_fusion.1), channel_id=1, replica_groups=mesh['dp'=8,'grp'=4] {'grp'}, use_global_device_ids=true, to_apply=%region_15.16 | all-reduce | flops 12800 | bytes 51200 | tf_op jit(solution)/shard_map/psum | solution.py:272
  1021.0 16.9 %all-reduce.56.cloned.1.call-done = (bf16[2,240,160]{1,2,0:T(8,128)(2,1)}, bf16[2,240,320]{1,2,0:T(8,128)(2,1)}, bf16[2,160,160]{1,2,0:T(8,128)(2,1)}, bf16[2,160,320]{2,0,1:T(2,128)(2,1)}) async-done(((bf16[2,240,160]{1,2,0:T(8,128)(2,1)}, bf16[2,240,320]{1,2,0:T(8,128)(2,1)}, bf16[2,160,160]{1,2,0:T(8,128)(2,1)}, bf16[2,160,320]{2,0,1:T(2,128)(2,1)}), (bf16[2,240,160]{1,2,0:T(8,128)(2,1)}, ...) | async-done | bytes 768016 | tf_op jit(solution)/shard_map/psum | solution.py:269
  1043.2 37.7 %all-reduce.50 = (f32[2,1120]{1,0:T(2,128)S(1)}, f32[2,1120]{1,0:T(2,128)}) all-reduce(f32[2,1120]{1,0:T(2,128)S(1)} %concatenate.97, f32[2,1120]{1,0:T(2,128)S(1)} %psum.62), channel_id=1, replica_groups=mesh['dp'=8,'grp'=4] {'dp'}, use_global_device_ids=true, to_apply=%region_20.21 | all-reduce | flops 4480 | bytes 35840 | tf_op jit(solution)/shard_map/psum | solution.py:282
  (488 shorter events, 407.0 us)
Async XLA Ops:
  7.2 99.0 %all-gather.4.cloned.1.call-start = ((), (), s32[]{:S(2)}) async-start(), calls=%async_computation.3 | async-start | bytes 2211840 | tf_op jit(solution)/shard_map/all_gather | solution.py:137
  9.1 130.0 %all-gather.8.cloned.1.call-start = ((), (), s32[]{:S(2)}) async-start(), calls=%async_computation.5 | async-start | bytes 2211840 | tf_op jit(solution)/shard_map/all_gather | solution.py:141
  9.9 170.5 %all-gather.6.cloned.1.call-start = ((), (), s32[]{:S(2)}) async-start(), calls=%async_computation.4 | async-start | bytes 3317760 | tf_op jit(solution)/shard_map/all_gather | solution.py:138
  11.8 982.9 %reduce-scatter.14.cloned.1.call-start = ((), (), s32[]{:S(2)}) async-start(), calls=%async_computation.8 | async-start | bytes 2211840
  102.7 18.7 %copy-start.16 = (bf16[3,32,32,320]{3,2,1,0:T(8,128)(2,1)}, bf16[3,32,32,320]{3,2,1,0:T(8,128)(2,1)S(1)}, u32[]{:S(2)}) copy-start(bf16[3,32,32,320]{3,2,1,0:T(8,128)(2,1)S(1)} %fusion.3) | copy-start | bytes 5898244
  114.6 12.1 %copy-start.109 = (f32[2,160]{1,0:T(2,128)}, f32[2,160]{1,0:T(2,128)S(1)}, u32[]{:S(2)}) copy-start(f32[2,160]{1,0:T(2,128)S(1)} %get-tuple-element.102) | copy-start | bytes 3844
  125.1 76.0 %copy-start.18 = (bf16[3,32,32,320]{3,2,1,0:T(8,128)(2,1)}, bf16[3,32,32,320]{3,2,1,0:T(8,128)(2,1)S(1)}, u32[]{:S(2)}) copy-start(bf16[3,32,32,320]{3,2,1,0:T(8,128)(2,1)S(1)} %fusion.5) | copy-start | bytes 5898244
  127.9 249.3 %copy-start.69 = (bf16[2,1280,160]{1,2,0:T(8,128)(2,1)}, bf16[2,1280,160]{1,2,0:T(8,128)(2,1)S(1)}, u32[]{:S(2)}) copy-start(bf16[2,1280,160]{1,2,0:T(8,128)(2,1)S(1)} %fusion.120) | copy-start | bytes 2457604
  183.7 76.5 %copy-start.101 = (f32[2,320]{1,0:T(2,128)}, f32[2,320]{1,0:T(2,128)S(1)}, u32[]{:S(2)}) copy-start(f32[2,320]{1,0:T(2,128)S(1)} %get-tuple-element.99) | copy-start | bytes 7684
  184.3 103.5 %copy-start.47 = (bf16[2,1920,320]{2,1,0:T(8,128)(2,1)}, bf16[2,1920,320]{2,1,0:T(8,128)(2,1)S(1)}, u32[]{:S(2)}) copy-start(bf16[2,1920,320]{2,1,0:T(8,128)(2,1)S(1)} %fusion.1) | copy-start | bytes 7372804
  211.2 85.7 %copy-start.33 = (f32[3,32,32,160]{3,2,1,0:T(8,128)}, f32[3,32,32,160]{3,2,1,0:T(8,128)S(1)}, u32[]{:S(2)}) copy-start(f32[3,32,32,160]{3,2,1,0:T(8,128)S(1)} %get-tuple-element.80) | copy-start | bytes 5898244
  213.4 38.4 %copy-start.5 = (bf16[3,32,32,320]{3,2,1,0:T(8,128)(2,1)}, bf16[3,32,32,320]{3,2,1,0:T(8,128)(2,1)S(1)}, u32[]{:S(2)}) copy-start(bf16[3,32,32,320]{3,2,1,0:T(8,128)(2,1)S(1)} %fusion.7) | copy-start | bytes 5898244
  233.0 54.8 %copy-start.20 = (bf16[3,32,32,320]{3,2,1,0:T(8,128)(2,1)}, bf16[3,32,32,320]{3,2,1,0:T(8,128)(2,1)S(1)}, u32[]{:S(2)}) copy-start(bf16[3,32,32,320]{3,2,1,0:T(8,128)(2,1)S(1)} %fusion.9) | copy-start | bytes 5898244
  274.5 48.0 %copy-start.39 = (f32[3,32,32,160]{3,2,1,0:T(8,128)}, f32[3,32,32,160]{3,2,1,0:T(8,128)S(1)}, u32[]{:S(2)}) copy-start(f32[3,32,32,160]{3,2,1,0:T(8,128)S(1)} %get-tuple-element.78) | copy-start | bytes 5898244
  361.3 19.0 %copy-start.12 = (bf16[3,32,32,160]{3,2,1,0:T(8,128)(2,1)}, bf16[3,32,32,160]{3,2,1,0:T(8,128)(2,1)S(1)}, u32[]{:S(2)}) copy-start(bf16[3,32,32,160]{3,2,1,0:T(8,128)(2,1)S(1)} %get-tuple-element.64) | copy-start | bytes 2949124
  383.4 26.2 %slice-start.2 = ((s8[4718592]{0:T(1024)(128)(4,1)}), s8[524288]{0:T(1024)(128)(4,1)S(1)}, s32[]{:S(2)}) async-start(s8[4718592]{0:T(1024)(128)(4,1)} %bitcast.644), calls=%async_computation.12 | async-start | bytes 1048576
  394.5 15.1 %slice-start.3 = ((s8[4718592]{0:T(1024)(128)(4,1)}), s8[4194304]{0:T(1024)(128)(4,1)S(1)}, s32[]{:S(2)}) async-start(s8[4718592]{0:T(1024)(128)(4,1)} %bitcast.644), calls=%async_computation.13 | async-start | bytes 8388608
  451.1 63.2 %copy-start.14 = (bf16[3,32,32,160]{3,2,1,0:T(8,128)(2,1)}, bf16[3,32,32,160]{3,2,1,0:T(8,128)(2,1)S(1)}, u32[]{:S(2)}) copy-start(bf16[3,32,32,160]{3,2,1,0:T(8,128)(2,1)S(1)} %get-tuple-element.56) | copy-start | bytes 2949124
  487.5 23.7 %copy-start.4 = (bf16[3,32,32,160]{3,2,1,0:T(8,128)(2,1)}, bf16[3,32,32,160]{3,2,1,0:T(8,128)(2,1)S(1)}, u32[]{:S(2)}) copy-start(bf16[3,32,32,160]{3,2,1,0:T(8,128)(2,1)S(1)} %get-tuple-element.68) | copy-start | bytes 2949124
  511.2 15.9 %slice-start = ((s8[4718592]{0:T(1024)(128)(4,1)}), s8[524288]{0:T(1024)(128)(4,1)S(1)}, s32[]{:S(2)}) async-start(s8[4718592]{0:T(1024)(128)(4,1)} %bitcast.642), calls=%async_computation.10 | async-start | bytes 1048576
  514.3 12.8 %slice-start.1 = ((s8[4718592]{0:T(1024)(128)(4,1)}), s8[4194304]{0:T(1024)(128)(4,1)S(1)}, s32[]{:S(2)}) async-start(s8[4718592]{0:T(1024)(128)(4,1)} %bitcast.642), calls=%async_computation.11 | async-start | bytes 8388608
  514.3 12.8 %copy-start.34 = (f32[3,32,32,160]{3,2,1,0:T(8,128)S(1)}, f32[3,32,32,160]{3,2,1,0:T(8,128)}, u32[]{:S(2)}) copy-start(f32[3,32,32,160]{3,2,1,0:T(8,128)} %copy-done.33) | copy-start | bytes 5898244
  514.3 13.8 %copy-start.45 = (f32[3,32,32,160]{3,2,1,0:T(8,128)S(1)}, f32[3,32,32,160]{3,2,1,0:T(8,128)}, u32[]{:S(2)}) copy-start(f32[3,32,32,160]{3,2,1,0:T(8,128)} %copy-done.44) | copy-start | bytes 5898244
  535.7 19.4 %copy-start = (bf16[3,32,32,320]{3,2,1,0:T(8,128)(2,1)}, bf16[3,32,32,320]{3,2,1,0:T(8,128)(2,1)S(1)}, u32[]{:S(2)}) copy-start(bf16[3,32,32,320]{3,2,1,0:T(8,128)(2,1)S(1)} %get-tuple-element.58) | copy-start | bytes 5898244
  574.5 422.3 %reduce-scatter.10.cloned.1.call-start = ((), (), s32[]{:S(2)}) async-start(), calls=%async_computation.6 | async-start | bytes 3317760
  619.1 379.7 %reduce-scatter.12.cloned.1.call-start = ((), (), s32[]{:S(2)}) async-start(), calls=%async_computation.7 | async-start | bytes 5529600
  682.2 355.7 %all-reduce.56.cloned.1.call-start = ((), (), s32[]{:S(2)}) async-start(), calls=%async_computation.9 | async-start | bytes 1802240 | tf_op jit(solution)/shard_map/psum | solution.py:269
  722.1 214.2 %copy-start.15 = (bf16[3,32,32,160]{3,2,1,0:T(8,128)(2,1)S(1)}, bf16[3,32,32,160]{3,2,1,0:T(8,128)(2,1)}, u32[]{:S(2)}) copy-start(bf16[3,32,32,160]{3,2,1,0:T(8,128)(2,1)} %copy-done.14) | copy-start | bytes 2949124
  722.1 214.2 %copy-start.70 = (bf16[2,1280,160]{1,2,0:T(8,128)(2,1)S(1)}, bf16[2,1280,160]{1,2,0:T(8,128)(2,1)}, u32[]{:S(2)}) copy-start(bf16[2,1280,160]{1,2,0:T(8,128)(2,1)} %copy-done.69) | copy-start | bytes 2457604
  973.8 13.3 %slice-start.6 = ((s8[6082560]{0:T(1024)(128)(4,1)}), s8[4194304]{0:T(1024)(128)(4,1)S(1)}, s32[]{:S(2)}) async-start(s8[6082560]{0:T(1024)(128)(4,1)} %bitcast.648), calls=%async_computation.16 | async-start | bytes 8388608
  994.7 26.2 %copy-start.93 = (bf16[2,40,160]{2,1,0:T(8,128)(2,1)S(1)}, bf16[2,40,160]{2,1,0:T(8,128)(2,1)}, u32[]{:S(2)}) copy-start(bf16[2,40,160]{2,1,0:T(8,128)(2,1)} %param.20) | copy-start | bytes 76804
  994.7 26.2 %copy-start.111 = (f32[2,160]{1,0:T(2,128)S(1)}, f32[2,160]{1,0:T(2,128)}, u32[]{:S(2)}) copy-start(f32[2,160]{1,0:T(2,128)} %get-tuple-element.108) | copy-start | bytes 3844
  994.7 43.3 %copy-start.78 = (bf16[2,240,160]{1,2,0:T(8,128)(2,1)S(1)}, bf16[2,240,160]{1,2,0:T(8,128)(2,1)}, u32[]{:S(2)}) copy-start(bf16[2,240,160]{1,2,0:T(8,128)(2,1)} %param.17) | copy-start | bytes 460804
  994.7 43.3 %copy-start.112 = (f32[2,160]{1,0:T(2,128)S(1)}, f32[2,160]{1,0:T(2,128)}, u32[]{:S(2)}) copy-start(f32[2,160]{1,0:T(2,128)} %get-tuple-element.106) | copy-start | bytes 3844
  994.7 44.5 %copy-start.76 = (bf16[2,240,320]{1,2,0:T(8,128)(2,1)S(1)}, bf16[2,240,320]{1,2,0:T(8,128)(2,1)}, u32[]{:S(2)}) copy-start(bf16[2,240,320]{1,2,0:T(8,128)(2,1)} %param.18) | copy-start | bytes 921604
  994.7 44.5 %copy-start.106 = (f32[2,320]{1,0:T(2,128)S(1)}, f32[2,320]{1,0:T(2,128)}, u32[]{:S(2)}) copy-start(f32[2,320]{1,0:T(2,128)} %get-tuple-element.104) | copy-start | bytes 7684
  994.7 45.8 %copy-start.77 = (bf16[2,160,320]{2,1,0:T(8,128)(2,1)S(1)}, bf16[2,160,320]{2,1,0:T(8,128)(2,1)}, u32[]{:S(2)}) copy-start(bf16[2,160,320]{2,1,0:T(8,128)(2,1)} %param.21) | copy-start | bytes 614404
  994.7 45.8 %copy-start.103 = (f32[2,320]{1,0:T(2,128)S(1)}, f32[2,320]{1,0:T(2,128)}, u32[]{:S(2)}) copy-start(f32[2,320]{1,0:T(2,128)} %get-tuple-element.105) | copy-start | bytes 7684
  994.7 47.2 %copy-start.79 = (bf16[2,160,160]{1,2,0:T(8,128)(2,1)S(1)}, bf16[2,160,160]{1,2,0:T(8,128)(2,1)}, u32[]{:S(2)}) copy-start(bf16[2,160,160]{1,2,0:T(8,128)(2,1)} %copy.39) | copy-start | bytes 307204
  994.7 47.2 %copy-start.113 = (f32[2,160]{1,0:T(2,128)S(1)}, f32[2,160]{1,0:T(2,128)}, u32[]{:S(2)}) copy-start(f32[2,160]{1,0:T(2,128)} %get-tuple-element.107) | copy-start | bytes 3844
  996.0 85.1 %copy-start.110 = (f32[2,160]{1,0:T(2,128)S(1)}, f32[2,160]{1,0:T(2,128)}, u32[]{:S(2)}) copy-start(f32[2,160]{1,0:T(2,128)} %copy-done.109) | copy-start | bytes 3844
  998.8 84.2 %copy-start.108 = (f32[2,160]{1,0:T(2,128)S(1)}, f32[2,160]{1,0:T(2,128)}, u32[]{:S(2)}) copy-start(f32[2,160]{1,0:T(2,128)} %copy-done.107) | copy-start | bytes 3844
  998.8 85.0 %copy-start.115 = (f32[2,160]{1,0:T(2,128)S(1)}, f32[2,160]{1,0:T(2,128)}, u32[]{:S(2)}) copy-start(f32[2,160]{1,0:T(2,128)} %copy-done.114) | copy-start | bytes 3844
  1000.2 84.5 %copy-start.102 = (f32[2,320]{1,0:T(2,128)S(1)}, f32[2,320]{1,0:T(2,128)}, u32[]{:S(2)}) copy-start(f32[2,320]{1,0:T(2,128)} %copy-done.101) | copy-start | bytes 7684
  1037.9 45.8 %copy-start.84 = (bf16[2,240,160]{1,2,0:T(8,128)(2,1)S(1)}, bf16[2,240,160]{1,2,0:T(8,128)(2,1)}, u32[]{:S(2)}) copy-start(bf16[2,240,160]{1,2,0:T(8,128)(2,1)} %get-tuple-element.49) | copy-start | bytes 460804
  1037.9 46.7 %copy-start.81 = (bf16[2,160,320]{2,0,1:T(2,128)(2,1)S(1)}, bf16[2,160,320]{2,0,1:T(2,128)(2,1)}, u32[]{:S(2)}) copy-start(bf16[2,160,320]{2,0,1:T(2,128)(2,1)} %get-tuple-element.52) | copy-start | bytes 614404
  1038.0 47.9 %copy-start.80 = (bf16[2,240,320]{1,2,0:T(8,128)(2,1)S(1)}, bf16[2,240,320]{1,2,0:T(8,128)(2,1)}, u32[]{:S(2)}) copy-start(bf16[2,240,320]{1,2,0:T(8,128)(2,1)} %get-tuple-element.50) | copy-start | bytes 921604
  1038.0 47.9 %copy-start.105 = (f32[2,320]{1,0:T(2,128)S(1)}, f32[2,320]{1,0:T(2,128)}, u32[]{:S(2)}) copy-start(f32[2,320]{1,0:T(2,128)} %copy-done.104) | copy-start | bytes 7684
  (91 other events, 455.0 us)
Sparse Core Ops, SparseCore 0:
  10.8 57.7 all-gather.3
  70.7 49.2 all-gather.7
  122.9 57.4 all-gather.5
  574.6 65.2 reduce-scatter.13
  643.7 71.3 reduce-scatter.9
  718.6 166.1 reduce-scatter.11
  1001.7 36.2 all-reduce.55
